TPU v7x, 768 devices: a whole 4x8x12 slice. The times are simulated.
768 devices in a mesh: outer: 24 (over y_hi, z), inner: 8 (over x, core), head: 4 (over y_lo).
Axes of the slice: x: 4, y: 8 (y_hi: 2, y_lo: 4; y = y_hi * 4 + y_lo), z: 12, core: 2. Of those that a mesh axis runs over, the one named last changes fastest.
Arguments:
- query: bfloat16 [24576, 6144], P(('outer', 'inner'), 'head'), may hold values from -6 to 6
- key: bfloat16 [24576, 1024], P(('outer', 'inner', 'head')), may hold values from -6 to 6
- value: bfloat16 [24576, 1024], P(('outer', 'inner', 'head')), may hold values from -6 to 6
- output_cotangent: bfloat16 [24576, 6144], P(('outer', 'inner'), 'head'), may hold values from -6 to 6
- segment: int32 [24576], replicated, may hold values from 0 to 191, never falling along the last dimension, each value on 1 to 256 neighbouring positions
Outputs:
- attended: bfloat16 [24576, 6144], P(('outer', 'inner'), 'head')
- d_query: bfloat16 [24576, 6144], P(('outer', 'inner'), 'head')
- d_key: bfloat16 [24576, 1024], P(('outer', 'inner', 'head'))
- d_value: bfloat16 [24576, 1024], P(('outer', 'inner', 'head'))
Inputs may be any that keep to these rules, and one draw needn't show every extreme that they name: `segment`: ids never fall along the row; every document has 1 to 256 tokens, and some document has exactly 256.
All inputs are finite; a program needn't handle non-finite values.
Results may differ from a plain program's by a relative error of at most 0.03.
Values may be sent and summed in bfloat16 or wider, within the bound.
No kernel may reach another device: no remote copies, remote signals or barrier semaphores. Data moves between devices by JAX's collectives and lax.ppermute only.
A program may use at most 32 MiB of HBM per device.

v0:
```python
import math

import jax
import jax.numpy as jnp
from jax import lax
from jax.sharding import PartitionSpec as P

QUERY_HEADS = 48
KEY_VALUE_HEADS = 8
HEAD_SIZE = 128
REACH = 2


def passed_along(x, axis, by):
    devices = lax.axis_size(axis)
    pairs = [(i, i + by) for i in range(devices) if 0 <= i + by < devices]
    return lax.ppermute(x, axis, pairs)


def block_allowed(query_seg, query_pos, segment, source, length):
    key_start = source * length
    key_seg = lax.dynamic_slice_in_dim(segment, jnp.maximum(key_start, 0), length, 0)
    key_pos = key_start + jnp.arange(length, dtype=jnp.int32)
    return (
        (query_seg[:, None] == key_seg[None, :])
        & (key_pos[None, :] <= query_pos[:, None])
        & (source >= 0)
    )


def block_scores(queries, block_key, allowed, factor):
    head_keys = block_key.reshape(block_key.shape[0], -1, HEAD_SIZE)
    scores = (
        jnp.einsum("tkgd,skd->kgts", queries, head_keys, preferred_element_type=jnp.float32)
        * factor
    )
    return jnp.where(allowed, scores, -jnp.inf)


def body(query, key, value, output_cotangent, segment):
    length = query.shape[0]
    query_group_width = QUERY_HEADS // KEY_VALUE_HEADS
    factor = 1.0 / math.sqrt(HEAD_SIZE)
    keys_here, values_here = (
        lax.all_to_all(key, "head", split_axis=1, concat_axis=0, tiled=True),
        lax.all_to_all(value, "head", split_axis=1, concat_axis=0, tiled=True),
    )
    kv_heads = keys_here.shape[1] // HEAD_SIZE
    shard_index = lax.axis_index(("outer", "inner"))
    first_row = shard_index * length
    query_seg = lax.dynamic_slice_in_dim(segment, first_row, length, 0)
    query_pos = first_row + jnp.arange(length, dtype=jnp.int32)
    queries = query.reshape(length, kv_heads, query_group_width, HEAD_SIZE)
    grads_out = output_cotangent.reshape(length, kv_heads, query_group_width, HEAD_SIZE)
    blocks = [(keys_here, values_here)]
    for offset in range(REACH):
        moved_key, moved_value = blocks[-1]
        blocks.append(passed_along((moved_key, moved_value), ("outer", "inner"), 1))
    masks = [
        block_allowed(query_seg, query_pos, segment, shard_index - offset, length)
        for offset in range(REACH + 1)
    ]
    row_max = None
    row_total = None
    for offset in range(REACH + 1):
        scores = block_scores(queries, blocks[offset][0], masks[offset], factor)
        block_max = jnp.max(scores, -1, keepdims=True)
        if offset == 0:
            row_max = block_max
            row_total = jnp.sum(jnp.exp(scores - row_max), -1, keepdims=True)
        else:
            new_max = jnp.maximum(row_max, block_max)
            row_total = row_total * jnp.exp(row_max - new_max) + jnp.sum(
                jnp.exp(scores - new_max), -1, keepdims=True
            )
            row_max = new_max
    log_total = row_max + jnp.log(row_total)
    attended_sum = jnp.zeros((length, kv_heads, query_group_width, HEAD_SIZE), jnp.float32)
    for offset in range(REACH + 1):
        block_key, block_value = blocks[offset]
        scores = block_scores(queries, block_key, masks[offset], factor)
        weights = jnp.exp(scores - log_total).astype(jnp.bfloat16)
        head_values = block_value.reshape(length, -1, HEAD_SIZE)
        attended_sum = attended_sum + jnp.einsum(
            "kgts,skd->tkgd", weights, head_values, preferred_element_type=jnp.float32
        )
    attended = attended_sum.astype(jnp.bfloat16)
    delta_row = jnp.sum(grads_out.astype(jnp.float32) * attended.astype(jnp.float32), -1)
    delta_row = jnp.transpose(delta_row, (1, 2, 0))[..., None]
    back_blocks = [(keys_here, values_here)]
    for offset in range(REACH):
        moved_key, moved_value = back_blocks[-1]
        back_blocks.append(passed_along((moved_key, moved_value), ("outer", "inner"), 1))
    grad_query = jnp.zeros((length, kv_heads, query_group_width, HEAD_SIZE), jnp.float32)
    partials = []
    for offset in range(REACH + 1):
        block_key, block_value = back_blocks[offset]
        head_keys = block_key.reshape(length, -1, HEAD_SIZE)
        head_values = block_value.reshape(length, -1, HEAD_SIZE)
        scores = block_scores(queries, block_key, masks[offset], factor)
        weights = jnp.exp(scores - log_total)
        weights_low = weights.astype(jnp.bfloat16)
        d_weights = jnp.einsum(
            "tkgd,skd->kgts", grads_out, head_values, preferred_element_type=jnp.float32
        )
        d_scores = (weights * (d_weights - delta_row)).astype(jnp.bfloat16)
        grad_query = grad_query + jnp.einsum(
            "kgts,skd->tkgd", d_scores, head_keys, preferred_element_type=jnp.float32
        )
        key_portion = (
            jnp.einsum("kgts,tkgd->skd", d_scores, queries, preferred_element_type=jnp.float32)
            * factor
        )
        value_portion = jnp.einsum(
            "kgts,tkgd->skd", weights_low, grads_out, preferred_element_type=jnp.float32
        )
        partials.append((key_portion.reshape(length, -1), value_portion.reshape(length, -1)))
    total_key, total_value = partials[REACH]
    for offset in range(REACH - 1, -1, -1):
        back_key, back_value = (
            passed_along(total_key.astype(jnp.bfloat16), ("outer", "inner"), -1).astype(
                total_key.dtype
            ),
            passed_along(total_value.astype(jnp.bfloat16), ("outer", "inner"), -1).astype(
                total_value.dtype
            ),
        )
        total_key = back_key + partials[offset][0]
        total_value = back_value + partials[offset][1]
    d_key, d_value = (
        lax.all_to_all(
            total_key.astype(jnp.bfloat16), "head", split_axis=0, concat_axis=1, tiled=True
        ),
        lax.all_to_all(
            total_value.astype(jnp.bfloat16), "head", split_axis=0, concat_axis=1, tiled=True
        ),
    )
    d_query = (grad_query * factor).astype(jnp.bfloat16).reshape(length, -1)
    return (attended.reshape(length, -1), d_query, d_key, d_value)


def solution(mesh):
    in_specs = (
        P(("outer", "inner"), "head"),
        P(("outer", "inner", "head"), None),
        P(("outer", "inner", "head"), None),
        P(("outer", "inner"), "head"),
        P(),
    )
    out_specs = (
        P(("outer", "inner"), "head"),
        P(("outer", "inner"), "head"),
        P(("outer", "inner", "head"), None),
        P(("outer", "inner", "head"), None),
    )
    return jax.shard_map(body, mesh=mesh, in_specs=in_specs, out_specs=out_specs, check_vma=False)
```

profile of v0, /device:TPU:56, one launch (start us, length us, event | category | flops | bytes accessed | tf_op | source)
XLA Modules:
  0.0 103.5 jit_solution(13492857087683430646)
XLA Ops:
  0.7 1.5 %copy.230 = bf16[4,4,8,256]{3,2,0,1:T(8,128)(2,1)} copy(bf16[4,4,8,256]{3,2,1,0:T(8,128)(2,1)} %bitcast.220) | data formatting | bytes 131072 | tf_op jit(solution)/shard_map/all_to_all | solution.py:45
  2.2 6.2 %all-to-all-start = ((bf16[32,4,256]{2,0,1:T(8,128)(2,1)}), bf16[32,4,256]{2,0,1:T(8,128)(2,1)S(1)}, u32[]{:S(2)}, u32[]{:S(2)}) async-start(bf16[32,4,256]{2,0,1:T(8,128)(2,1)} %bitcast.178), calls=%async_computation | async-start | bytes 131072 | tf_op jit(solution)/shard_map/all_to_all | solution.py:45
  9.0 0.9 fusion.36
  9.9 1.1 %all-to-all-done = bf16[32,4,256]{2,0,1:T(8,128)(2,1)S(1)} async-done(((bf16[32,4,256]{2,0,1:T(8,128)(2,1)}), bf16[32,4,256]{2,0,1:T(8,128)(2,1)S(1)}, u32[]{:S(2)}, u32[]{:S(2)}) %all-to-all-start) | async-done | bytes 65568 | tf_op jit(solution)/shard_map/all_to_all | solution.py:45
  11.0 6.3 %all-to-all-start.1 = ((bf16[32,4,256]{2,0,1:T(8,128)(2,1)}), bf16[32,4,256]{2,0,1:T(8,128)(2,1)S(1)}, u32[]{:S(2)}, u32[]{:S(2)}) async-start(bf16[32,4,256]{2,0,1:T(8,128)(2,1)} %bitcast.179), calls=%async_computation.1 | async-start | bytes 131072 | tf_op jit(solution)/shard_map/all_to_all | solution.py:46
  17.8 0.8 copy-done.16
  18.9 1.1 %all-to-all-done.1 = bf16[32,4,256]{2,0,1:T(8,128)(2,1)S(1)} async-done(((bf16[32,4,256]{2,0,1:T(8,128)(2,1)}), bf16[32,4,256]{2,0,1:T(8,128)(2,1)S(1)}, u32[]{:S(2)}, u32[]{:S(2)}) %all-to-all-start.1) | async-done | bytes 65568 | tf_op jit(solution)/shard_map/all_to_all | solution.py:46
  20.0 1.9 %collective-permute-start.2 = (bf16[128,256]{1,0:T(8,128)(2,1)S(1)}, bf16[128,256]{1,0:T(8,128)(2,1)S(1)}, u32[]{:S(2)}, u32[]{:S(2)}) collective-permute-start(bf16[128,256]{1,0:T(8,128)(2,1)S(1)} %bitcast.210), channel_id=1, source_target_pairs={{0,4},{4,8},{8,12},{12,16},{16,20},{20,24},{24,28},{28,32},{32,36}... | collective-permute-start | bytes 196616 | tf_op jit(solution)/shard_map/ppermute | solution.py:17
  21.9 3.5 %collective-permute-start = (bf16[128,256]{1,0:T(8,128)(2,1)S(1)}, bf16[128,256]{1,0:T(8,128)(2,1)S(1)}, u32[]{:S(2)}, u32[]{:S(2)}) collective-permute-start(bf16[128,256]{1,0:T(8,128)(2,1)S(1)} %bitcast.209), channel_id=1, source_target_pairs={{0,4},{4,8},{8,12},{12,16},{16,20},{20,24},{24,28},{28,32},{32,36}... | collective-permute-start | bytes 196616 | tf_op jit(solution)/shard_map/ppermute | solution.py:17
  26.1 13.5 %collective-permute-done = bf16[128,256]{1,0:T(8,128)(2,1)S(1)} collective-permute-done((bf16[128,256]{1,0:T(8,128)(2,1)S(1)}, bf16[128,256]{1,0:T(8,128)(2,1)S(1)}, u32[]{:S(2)}, u32[]{:S(2)}) %collective-permute-start) | collective-permute-done | bytes 65568 | tf_op jit(solution)/shard_map/ppermute | solution.py:17
  39.7 1.9 %collective-permute-start.1 = (bf16[128,256]{1,0:T(8,128)(2,1)S(1)}, bf16[128,256]{1,0:T(8,128)(2,1)S(1)}, u32[]{:S(2)}, u32[]{:S(2)}) collective-permute-start(bf16[128,256]{1,0:T(8,128)(2,1)S(1)} %collective-permute-done), channel_id=1, source_target_pairs={{0,4},{4,8},{8,12},{12,16},{16,20},{20,24},{24,28},{28,32},{32,36}... | collective-permute-start | bytes 196616 | tf_op jit(solution)/shard_map/ppermute | solution.py:17
  42.1 1.9 %collective-permute-start.3 = (bf16[128,256]{1,0:T(8,128)(2,1)S(1)}, bf16[128,256]{1,0:T(8,128)(2,1)S(1)}, u32[]{:S(2)}, u32[]{:S(2)}) collective-permute-start(bf16[128,256]{1,0:T(8,128)(2,1)S(1)} %collective-permute-done.2), channel_id=1, source_target_pairs={{0,4},{4,8},{8,12},{12,16},{16,20},{20,24},{24,28},{28,32},{32,36}... | collective-permute-start | bytes 196616 | tf_op jit(solution)/shard_map/ppermute | solution.py:17
  44.0 10.0 %collective-permute-done.1 = bf16[128,256]{1,0:T(8,128)(2,1)S(1)} collective-permute-done((bf16[128,256]{1,0:T(8,128)(2,1)S(1)}, bf16[128,256]{1,0:T(8,128)(2,1)S(1)}, u32[]{:S(2)}, u32[]{:S(2)}) %collective-permute-start.1) | collective-permute-done | bytes 65568 | tf_op jit(solution)/shard_map/ppermute | solution.py:17
  55.1 0.9 fusion.31
  56.0 0.9 fusion.28
  57.2 1.2 %convolution_add_fusion.3 = f32[2,6,128,128]{2,3,1,0:T(8,128)} fusion(f32[2,6,128,128]{2,3,1,0:T(8,128)S(1)} %fusion.33, bf16[128,2,128,1]{0,2,3,1:T(8,128)(2,1)S(1)} %bitcast.199, f32[2,6,128,128]{2,3,1,0:T(8,128)S(1)} %get-tuple-element.34, f32[2,6,128]{2,1,0:T(8,128)S(1)} %log_add_fusion), kind=kOutput, calls=%fused_computation.4 | convolution fusion | flops 50921472 | bytes 2430976 | tf_op jit(solution)/shard_map/kgts,skd->tkgd/dot_general | solution.py:84
  58.4 0.9 fusion.22
  59.5 2.2 %multiply_reduce_fusion = (f32[128,2,6]{0,2,1:T(8,128)S(1)}, bf16[2,6,128,128]{2,3,1,0:T(8,128)(2,1)}) fusion(bf16[128,2,6,128]{0,3,2,1:T(8,128)(2,1)S(1)} %bitcast.183, f32[2,6,128,128]{2,3,1,0:T(8,128)} %convolution_add_fusion.3, bf16[128,2,128,1]{0,2,3,1:T(8,128)(2,1)S(1)} %bitcast.201, f32[2,6,128,128]{2,3,1,0:T(8,128)S(1)} %get-tuple-element.30, ...), kind=kOutput, calls=%fused_computation.37 | convolution fusion | flops 51902976 | bytes 2437120 | tf_op jit(solution)/shard_map/kgts,skd->tkgd/dot_general | solution.py:84
  65.5 1.9 %collective-permute-start.6 = (bf16[128,256]{1,0:T(8,128)(2,1)S(1)}, bf16[128,256]{1,0:T(8,128)(2,1)S(1)}, u32[]{:S(2)}, u32[]{:S(2)}) collective-permute-start(bf16[128,256]{1,0:T(8,128)(2,1)S(1)} %copy.164), channel_id=1, source_target_pairs={{4,0},{8,4},{12,8},{16,12},{20,16},{24,20},{28,24},{32,28},{36,32}... | collective-permute-start | bytes 196616 | tf_op jit(solution)/shard_map/ppermute | solution.py:17
  67.8 2.3 %collective-permute-start.4 = (bf16[128,256]{1,0:T(8,128)(2,1)S(1)}, bf16[128,256]{1,0:T(8,128)(2,1)S(1)}, u32[]{:S(2)}, u32[]{:S(2)}) collective-permute-start(bf16[128,256]{1,0:T(8,128)(2,1)S(1)} %copy.157), channel_id=1, source_target_pairs={{4,0},{8,4},{12,8},{16,12},{20,16},{24,20},{28,24},{32,28},{36,32}... | collective-permute-start | bytes 196616 | tf_op jit(solution)/shard_map/ppermute | solution.py:17
  71.4 0.8 copy-done.13
  72.5 9.2 %collective-permute-start.7 = (bf16[128,256]{1,0:T(8,128)(2,1)S(1)}, bf16[128,256]{1,0:T(8,128)(2,1)S(1)}, u32[]{:S(2)}, u32[]{:S(2)}) collective-permute-start(bf16[128,256]{1,0:T(8,128)(2,1)S(1)} %add_convert_fusion.1), channel_id=1, source_target_pairs={{4,0},{8,4},{12,8},{16,12},{20,16},{24,20},{28,24},{32,28},{36,32}... | collective-permute-start | bytes 196616 | tf_op jit(solution)/shard_map/ppermute | solution.py:17
  81.8 2.6 %collective-permute-start.5 = (bf16[128,256]{1,0:T(8,128)(2,1)S(1)}, bf16[128,256]{1,0:T(8,128)(2,1)S(1)}, u32[]{:S(2)}, u32[]{:S(2)}) collective-permute-start(bf16[128,256]{1,0:T(8,128)(2,1)S(1)} %add_convert_fusion.3), channel_id=1, source_target_pairs={{4,0},{8,4},{12,8},{16,12},{20,16},{24,20},{28,24},{32,28},{36,32}... | collective-permute-start | bytes 196616 | tf_op jit(solution)/shard_map/ppermute | solution.py:17
  84.5 0.6 add_convert_fusion
  85.1 5.1 %all-to-all-start.3 = ((bf16[4,32,256]{2,1,0:T(8,128)(2,1)}), bf16[4,32,256]{2,1,0:T(8,128)(2,1)S(1)}, u32[]{:S(2)}, u32[]{:S(2)}) async-start(bf16[4,32,256]{2,1,0:T(8,128)(2,1)} %bitcast.63), calls=%async_computation.3 | async-start | bytes 131072 | tf_op jit(solution)/shard_map/all_to_all | solution.py:134
  90.2 0.6 add_convert_fusion.2
  90.9 2.0 %all-to-all-done.3 = bf16[4,32,256]{2,1,0:T(8,128)(2,1)S(1)} async-done(((bf16[4,32,256]{2,1,0:T(8,128)(2,1)}), bf16[4,32,256]{2,1,0:T(8,128)(2,1)S(1)}, u32[]{:S(2)}, u32[]{:S(2)}) %all-to-all-start.3) | async-done | bytes 65568 | tf_op jit(solution)/shard_map/all_to_all | solution.py:134
  92.9 6.5 %all-to-all-start.2 = ((bf16[4,32,256]{2,1,0:T(8,128)(2,1)}), bf16[4,32,256]{2,1,0:T(8,128)(2,1)S(1)}, u32[]{:S(2)}, u32[]{:S(2)}) async-start(bf16[4,32,256]{2,1,0:T(8,128)(2,1)} %bitcast.49), calls=%async_computation.2 | async-start | bytes 131072 | tf_op jit(solution)/shard_map/all_to_all | solution.py:131
  99.6 0.7 copy-done
  100.4 0.9 copy.170
  101.3 0.9 copy.171
  102.8 0.6 copy.226
  (82 shorter events, 10.5 us)
Async XLA Ops:
  0.6 7.7 %copy-start.18 = (bf16[32,1024]{1,0:T(8,128)(2,1)S(1)}, bf16[32,1024]{1,0:T(8,128)(2,1)}, u32[]{:S(2)}) copy-start(bf16[32,1024]{1,0:T(8,128)(2,1)} %param.7) | copy-start | bytes 196612
  0.6 16.9 %copy-start.15 = (bf16[128,1536]{1,0:T(8,128)(2,1)S(1)}, bf16[128,1536]{1,0:T(8,128)(2,1)}, u32[]{:S(2)}) copy-start(bf16[128,1536]{1,0:T(8,128)(2,1)} %param.5) | copy-start | bytes 1179652
  2.2 8.8 %all-to-all-start = ((bf16[32,4,256]{2,0,1:T(8,128)(2,1)}), bf16[32,4,256]{2,0,1:T(8,128)(2,1)S(1)}, u32[]{:S(2)}, u32[]{:S(2)}) async-start(bf16[32,4,256]{2,0,1:T(8,128)(2,1)} %bitcast.178), calls=%async_computation | async-start | bytes 131072 | tf_op jit(solution)/shard_map/all_to_all | solution.py:45
  11.0 9.0 %all-to-all-start.1 = ((bf16[32,4,256]{2,0,1:T(8,128)(2,1)}), bf16[32,4,256]{2,0,1:T(8,128)(2,1)S(1)}, u32[]{:S(2)}, u32[]{:S(2)}) async-start(bf16[32,4,256]{2,0,1:T(8,128)(2,1)} %bitcast.179), calls=%async_computation.1 | async-start | bytes 131072 | tf_op jit(solution)/shard_map/all_to_all | solution.py:46
  17.5 1.0 copy-start.16
  18.9 6.9 %copy-start.3 = (bf16[128,2,128,1]{0,2,3,1:T(8,128)(2,1)}, bf16[128,2,128,1]{0,2,3,1:T(8,128)(2,1)S(1)}, u32[]{:S(2)}) copy-start(bf16[128,2,128,1]{0,2,3,1:T(8,128)(2,1)S(1)} %copy.187) | copy-start | bytes 196612
  20.0 21.9 %collective-permute-start.2 = (bf16[128,256]{1,0:T(8,128)(2,1)S(1)}, bf16[128,256]{1,0:T(8,128)(2,1)S(1)}, u32[]{:S(2)}, u32[]{:S(2)}) collective-permute-start(bf16[128,256]{1,0:T(8,128)(2,1)S(1)} %bitcast.210), channel_id=1, source_target_pairs={{0,4},{4,8},{8,12},{12,16},{16,20},{20,24},{24,28},{28,32},{32,36}... | collective-permute-start | bytes 196616 | tf_op jit(solution)/shard_map/ppermute | solution.py:17
  21.9 17.6 %collective-permute-start = (bf16[128,256]{1,0:T(8,128)(2,1)S(1)}, bf16[128,256]{1,0:T(8,128)(2,1)S(1)}, u32[]{:S(2)}, u32[]{:S(2)}) collective-permute-start(bf16[128,256]{1,0:T(8,128)(2,1)S(1)} %bitcast.209), channel_id=1, source_target_pairs={{0,4},{4,8},{8,12},{12,16},{16,20},{20,24},{24,28},{28,32},{32,36}... | collective-permute-start | bytes 196616 | tf_op jit(solution)/shard_map/ppermute | solution.py:17
  26.1 30.9 %copy-start.7 = (bf16[128,2,128,1]{0,2,3,1:T(8,128)(2,1)}, bf16[128,2,128,1]{0,2,3,1:T(8,128)(2,1)S(1)}, u32[]{:S(2)}) copy-start(bf16[128,2,128,1]{0,2,3,1:T(8,128)(2,1)S(1)} %copy.179) | copy-start | bytes 196612
  39.7 2.3 %copy-start.5 = (bf16[128,256]{0,1:T(8,128)(2,1)}, bf16[128,256]{0,1:T(8,128)(2,1)S(1)}, u32[]{:S(2)}) copy-start(bf16[128,256]{0,1:T(8,128)(2,1)S(1)} %copy.132) | copy-start | bytes 196612
  39.7 14.3 %collective-permute-start.1 = (bf16[128,256]{1,0:T(8,128)(2,1)S(1)}, bf16[128,256]{1,0:T(8,128)(2,1)S(1)}, u32[]{:S(2)}, u32[]{:S(2)}) collective-permute-start(bf16[128,256]{1,0:T(8,128)(2,1)S(1)} %collective-permute-done), channel_id=1, source_target_pairs={{0,4},{4,8},{8,12},{12,16},{16,20},{20,24},{24,28},{28,32},{32,36}... | collective-permute-start | bytes 196616 | tf_op jit(solution)/shard_map/ppermute | solution.py:17
  42.1 15.2 %copy-start.9 = (bf16[128,256]{0,1:T(8,128)(2,1)}, bf16[128,256]{0,1:T(8,128)(2,1)S(1)}, u32[]{:S(2)}) copy-start(bf16[128,256]{0,1:T(8,128)(2,1)S(1)} %copy.141) | copy-start | bytes 196612
  42.1 17.3 %collective-permute-start.3 = (bf16[128,256]{1,0:T(8,128)(2,1)S(1)}, bf16[128,256]{1,0:T(8,128)(2,1)S(1)}, u32[]{:S(2)}, u32[]{:S(2)}) collective-permute-start(bf16[128,256]{1,0:T(8,128)(2,1)S(1)} %collective-permute-done.2), channel_id=1, source_target_pairs={{0,4},{4,8},{8,12},{12,16},{16,20},{20,24},{24,28},{28,32},{32,36}... | collective-permute-start | bytes 196616 | tf_op jit(solution)/shard_map/ppermute | solution.py:17
  54.1 0.6 copy-start.1
  59.5 2.3 %copy-start.11 = (bf16[128,256]{0,1:T(8,128)(2,1)}, bf16[128,256]{0,1:T(8,128)(2,1)S(1)}, u32[]{:S(2)}) copy-start(bf16[128,256]{0,1:T(8,128)(2,1)S(1)} %copy.143) | copy-start | bytes 196612
  59.5 2.2 %copy-start.10 = (bf16[128,256]{0,1:T(8,128)(2,1)S(1)}, bf16[128,256]{0,1:T(8,128)(2,1)}, u32[]{:S(2)}) copy-start(bf16[128,256]{0,1:T(8,128)(2,1)} %copy-done.9) | copy-start | bytes 196612
  61.7 0.8 copy-start.12
  62.6 0.8 copy-start.8
  63.7 0.8 copy-start.4
  64.6 0.8 copy-start.17
  65.5 7.0 %collective-permute-start.6 = (bf16[128,256]{1,0:T(8,128)(2,1)S(1)}, bf16[128,256]{1,0:T(8,128)(2,1)S(1)}, u32[]{:S(2)}, u32[]{:S(2)}) collective-permute-start(bf16[128,256]{1,0:T(8,128)(2,1)S(1)} %copy.164), channel_id=1, source_target_pairs={{4,0},{8,4},{12,8},{16,12},{20,16},{24,20},{28,24},{32,28},{36,32}... | collective-permute-start | bytes 196616 | tf_op jit(solution)/shard_map/ppermute | solution.py:17
  67.7 2.4 %copy-start.6 = (bf16[128,256]{0,1:T(8,128)(2,1)S(1)}, bf16[128,256]{0,1:T(8,128)(2,1)}, u32[]{:S(2)}) copy-start(bf16[128,256]{0,1:T(8,128)(2,1)} %copy-done.5) | copy-start | bytes 196612
  67.8 14.0 %collective-permute-start.4 = (bf16[128,256]{1,0:T(8,128)(2,1)S(1)}, bf16[128,256]{1,0:T(8,128)(2,1)S(1)}, u32[]{:S(2)}, u32[]{:S(2)}) collective-permute-start(bf16[128,256]{1,0:T(8,128)(2,1)S(1)} %copy.157), channel_id=1, source_target_pairs={{4,0},{8,4},{12,8},{16,12},{20,16},{24,20},{28,24},{32,28},{36,32}... | collective-permute-start | bytes 196616 | tf_op jit(solution)/shard_map/ppermute | solution.py:17
  70.4 0.9 copy-start.14
  71.3 0.9 copy-start.13
  72.5 11.9 %collective-permute-start.7 = (bf16[128,256]{1,0:T(8,128)(2,1)S(1)}, bf16[128,256]{1,0:T(8,128)(2,1)S(1)}, u32[]{:S(2)}, u32[]{:S(2)}) collective-permute-start(bf16[128,256]{1,0:T(8,128)(2,1)S(1)} %add_convert_fusion.1), channel_id=1, source_target_pairs={{4,0},{8,4},{12,8},{16,12},{20,16},{24,20},{28,24},{32,28},{36,32}... | collective-permute-start | bytes 196616 | tf_op jit(solution)/shard_map/ppermute | solution.py:17
  81.8 8.4 %collective-permute-start.5 = (bf16[128,256]{1,0:T(8,128)(2,1)S(1)}, bf16[128,256]{1,0:T(8,128)(2,1)S(1)}, u32[]{:S(2)}, u32[]{:S(2)}) collective-permute-start(bf16[128,256]{1,0:T(8,128)(2,1)S(1)} %add_convert_fusion.3), channel_id=1, source_target_pairs={{4,0},{8,4},{12,8},{16,12},{20,16},{24,20},{28,24},{32,28},{36,32}... | collective-permute-start | bytes 196616 | tf_op jit(solution)/shard_map/ppermute | solution.py:17
  85.1 7.8 %all-to-all-start.3 = ((bf16[4,32,256]{2,1,0:T(8,128)(2,1)}), bf16[4,32,256]{2,1,0:T(8,128)(2,1)S(1)}, u32[]{:S(2)}, u32[]{:S(2)}) async-start(bf16[4,32,256]{2,1,0:T(8,128)(2,1)} %bitcast.63), calls=%async_computation.3 | async-start | bytes 131072 | tf_op jit(solution)/shard_map/all_to_all | solution.py:134
  92.9 6.5 %copy-start.2 = (bf16[128,256]{0,1:T(8,128)(2,1)S(1)}, bf16[128,256]{0,1:T(8,128)(2,1)}, u32[]{:S(2)}) copy-start(bf16[128,256]{0,1:T(8,128)(2,1)} %copy-done.1) | copy-start | bytes 196612
  92.9 10.0 %all-to-all-start.2 = ((bf16[4,32,256]{2,1,0:T(8,128)(2,1)}), bf16[4,32,256]{2,1,0:T(8,128)(2,1)S(1)}, u32[]{:S(2)}, u32[]{:S(2)}) async-start(bf16[4,32,256]{2,1,0:T(8,128)(2,1)} %bitcast.49), calls=%async_computation.2 | async-start | bytes 131072 | tf_op jit(solution)/shard_map/all_to_all | solution.py:131
  99.4 1.0 copy-start
where the time goes:
time: 105 us; the launch traced here: 103 us
  starting transfers between devices  49.4 us (47%)
  waiting for transfers between devices  27.7 us (26%)
  local copies, waits for them, and re-layouts  12.5 us (12%)
  matrix products  9.94 us (9%)
  other arithmetic  2.81 us (3%)
  between operations  1.14 us (1%)
    ppermute x8, starting transfers between devices, passed_along(): return lax.ppermute(x, axis, pairs)  25.3 us
    ppermute x8, waiting for transfers between devices, passed_along(): return lax.ppermute(x, axis, pairs)  23.5 us
    unnamed x42, local copies, waits for them, and re-layouts  7.75 us
    all_to_all x1, starting transfers between devices, body(): lax.all_to_all(total_key.astype(jnp.bfloat16), 'head', split_axis=0, conc...  6.47 us
    all_to_all x1, starting transfers between devices, body(): lax.all_to_all(value, 'head', split_axis=1, concat_axis=0, tiled=True)  6.34 us
    all_to_all x1, starting transfers between devices, body(): lax.all_to_all(key, 'head', split_axis=1, concat_axis=0, tiled=True)  6.18 us
    all_to_all x1, starting transfers between devices, body(): lax.all_to_all(total_value.astype(jnp.bfloat16), 'head', split_axis=0, co...  5.09 us
    dot_general x3, matrix products, body(): jnp.einsum('kgts,skd->tkgd', weights, head_values, preferred_element_type...  3.68 us
  transfers between devices with their start and end apart: 12, of which 5 were waited for; matrix products, arithmetic and copies ran while one was open for 13% of the time, Pallas kernels for 0%

commit v1 on v0

v1 whole, which is shorter than its diff:
```python
import math

import jax
import jax.numpy as jnp
from jax import lax
from jax.experimental import pallas as pl
from jax.experimental.pallas import tpu as pltpu
from jax.sharding import PartitionSpec as P

QUERY_HEADS = 48
KEY_VALUE_HEADS = 8
HEAD_SIZE = 128
GROUP = QUERY_HEADS // KEY_VALUE_HEADS
REACH = 2
TOKENS = 128
SHARDS = ("outer", "inner")
FACTOR = 1.0 / math.sqrt(HEAD_SIZE)
LOG2E = math.log2(math.e)
FAR = -1e30


def passed_along(x, by):
    devices = lax.axis_size(SHARDS)
    pairs = [(i, i + by) for i in range(devices) if 0 <= i + by < devices]
    return lax.ppermute(x, SHARDS, pairs)


def exchanged(x):
    return lax.all_to_all(x, "head", split_axis=0, concat_axis=0, tiled=True)


def nt(a, b):
    return lax.dot_general(a, b, (((1,), (1,)), ((), ())), preferred_element_type=jnp.float32)


def nn(a, b):
    return jnp.dot(a, b, preferred_element_type=jnp.float32)


def attention(
    q_ref, g_ref, kv0_ref, kv1_ref, kv2_ref, bias_ref,
    att_ref, dq_ref, own_ref, back1_ref, back2_ref, p_ref, s_ref,
):
    upper = lax.broadcasted_iota(jnp.int32, (TOKENS, TOKENS), 0) <= lax.broadcasted_iota(
        jnp.int32, (TOKENS, TOKENS), 1
    )
    for g in range(kv0_ref.shape[-1] // HEAD_SIZE):
        columns = slice(g * HEAD_SIZE, (g + 1) * HEAD_SIZE)
        keys, values = (
            [ref[:, w, :, columns].reshape(TOKENS, HEAD_SIZE) for ref in (kv2_ref, kv1_ref, kv0_ref)]
            for w in range(2)
        )
        key_rows, value_rows = jnp.concatenate(keys, 0), jnp.concatenate(values, 0)
        key_columns = jnp.concatenate([k.T for k in keys], 1)
        value_columns = jnp.concatenate([v.T for v in values], 1)
        for j in range(GROUP):
            at = slice((g * GROUP + j) * HEAD_SIZE, (g * GROUP + j + 1) * HEAD_SIZE)
            lanes = slice(j * TOKENS, (j + 1) * TOKENS)
            scores = nt(key_rows, q_ref[:, at])
            d_weights = nt(value_rows, g_ref[:, at])
            sa = jnp.where(upper, scores[2 * TOKENS :], scores[:TOKENS]) * (FACTOR * LOG2E) + bias_ref[0]
            sb = scores[TOKENS : 2 * TOKENS] * (FACTOR * LOG2E) + bias_ref[1]
            top = jnp.max(jnp.maximum(sa, sb), 0, keepdims=True)
            pa, pb = jnp.exp2(sa - top), jnp.exp2(sb - top)
            scale = 1.0 / jnp.sum(pa + pb, 0, keepdims=True)
            pa, pb = pa * scale, pb * scale
            da = jnp.where(upper, d_weights[2 * TOKENS :], d_weights[:TOKENS])
            db = d_weights[TOKENS : 2 * TOKENS]
            delta = jnp.sum(pa * da + pb * db, 0, keepdims=True)
            ea, eb = pa * (da - delta), pb * (db - delta)
            for ref, a, b in ((p_ref, pa, pb), (s_ref, ea, eb)):
                ref[:TOKENS, lanes] = jnp.where(upper, 0.0, a).astype(jnp.bfloat16)
                ref[TOKENS : 2 * TOKENS, lanes] = b.astype(jnp.bfloat16)
                ref[2 * TOKENS :, lanes] = jnp.where(upper, a, 0.0).astype(jnp.bfloat16)
        heads = [
            slice((g * GROUP + j) * HEAD_SIZE, (g * GROUP + j + 1) * HEAD_SIZE) for j in range(GROUP)
        ]
        queries = jnp.concatenate([q_ref[:, at] for at in heads], 0)
        cotangents = jnp.concatenate([g_ref[:, at] for at in heads], 0)
        d_key = nn(s_ref[...], queries) * FACTOR
        d_value = nn(p_ref[...], cotangents)
        for ref, first in ((back2_ref, 0), (back1_ref, TOKENS), (own_ref, 2 * TOKENS)):
            for w, grad in ((0, d_key), (1, d_value)):
                part = grad[first : first + TOKENS].astype(ref.dtype)
                ref[:, w, :, columns] = part.reshape(ref.shape[0], ref.shape[2], HEAD_SIZE)
        attended = nn(value_columns, p_ref[...])
        d_query = nn(key_columns, s_ref[...]) * FACTOR
        for j, at in enumerate(heads):
            lanes = slice(j * TOKENS, (j + 1) * TOKENS)
            att_ref[:, at] = attended[:, lanes].T.astype(jnp.bfloat16)
            dq_ref[:, at] = d_query[:, lanes].T.astype(jnp.bfloat16)


def pack(k_ref, v_ref, x_ref):
    width = x_ref.shape[-1]
    for c in range(x_ref.shape[0]):
        x_ref[c, 0] = k_ref[:, c * width : (c + 1) * width]
        x_ref[c, 1] = v_ref[:, c * width : (c + 1) * width]


def finish(x_ref, dk_ref, dv_ref):
    width = x_ref.shape[-1]
    for c in range(x_ref.shape[0]):
        dk_ref[:, c * width : (c + 1) * width] = x_ref[c, 0]
        dv_ref[:, c * width : (c + 1) * width] = x_ref[c, 1]


def body(query, key, value, output_cotangent, segment):
    length = query.shape[0]
    rows, width = key.shape
    members = length // rows
    width //= members
    vmem = pl.BlockSpec(memory_space=pltpu.VMEM)
    out = jax.ShapeDtypeStruct
    packed = pl.pallas_call(
        pack,
        out_shape=out((members, 2, rows, width), key.dtype),
        in_specs=[vmem] * 2,
        out_specs=vmem,
        name="pack",
    )(key, value)
    blocks = [exchanged(packed)]
    for offset in range(1, REACH + 1):
        blocks.append(passed_along(blocks[0], offset))

    shard = lax.axis_index(SHARDS)
    segments = []
    for offset in range(REACH + 1):
        source = shard - offset
        part = lax.dynamic_slice_in_dim(segment, jnp.maximum(source, 0) * length, length, 0)
        segments.append(jnp.where(source >= 0, part, -1))
    upper = jnp.arange(length)[:, None] <= jnp.arange(length)[None, :]
    mine = segments[0][None, :]
    meets = jnp.stack(
        [
            jnp.where(upper, segments[0][:, None], segments[2][:, None]) == mine,
            segments[1][:, None] == mine,
        ]
    )
    bias = jnp.where(meets, 0.0, FAR)

    block = blocks[0].shape
    attended, d_query, own, back1, back2 = pl.pallas_call(
        attention,
        out_shape=(
            out(query.shape, query.dtype),
            out(query.shape, query.dtype),
            out(block, jnp.float32),
            out(block, jnp.bfloat16),
            out(block, jnp.bfloat16),
        ),
        in_specs=[vmem] * 6,
        out_specs=[vmem] * 5,
        scratch_shapes=[pltpu.VMEM((3 * TOKENS, GROUP * TOKENS), jnp.bfloat16)] * 2,
        compiler_params=pltpu.CompilerParams(vmem_limit_bytes=24 * 1024 * 1024),
        name="attention",
    )(query, output_cotangent, *blocks, bias)

    back = [passed_along(back1, -1), passed_along(back2, -2)]
    total = own + back[0].astype(jnp.float32) + back[1].astype(jnp.float32)
    gathered = exchanged(total.astype(jnp.bfloat16))
    d_key, d_value = pl.pallas_call(
        finish,
        out_shape=(out(key.shape, key.dtype), out(value.shape, value.dtype)),
        in_specs=[vmem],
        out_specs=[vmem] * 2,
        name="finish",
    )(gathered)
    return attended, d_query, d_key, d_value


def solution(mesh):
    in_specs = (
        P(("outer", "inner"), "head"),
        P(("outer", "inner", "head"), None),
        P(("outer", "inner", "head"), None),
        P(("outer", "inner"), "head"),
        P(),
    )
    out_specs = (
        P(("outer", "inner"), "head"),
        P(("outer", "inner"), "head"),
        P(("outer", "inner", "head"), None),
        P(("outer", "inner", "head"), None),
    )
    return jax.shard_map(body, mesh=mesh, in_specs=in_specs, out_specs=out_specs, check_vma=False)
```

time: 105 us -> 61.4 us (0.58)
  starting transfers between devices: 49.4 us -> 15.4 us
  local copies, waits for them, and re-layouts: 12.5 us -> 0.01 us
  matrix products: 9.94 us -> 0 us
  blocking collectives: 0 us -> 8.5 us
  Pallas kernels: 0 us -> 6.75 us
  other arithmetic: 2.81 us -> 1.03 us
    all_to_all x4 -> x1, starting transfers between devices: 24.1 us -> 6.22 us  [exchanged(): return lax.all_to_all(x, 'head', split_axis=0, concat_axis=0, tiled=True)]
    ppermute x8 -> x4, starting transfers between devices: 25.3 us -> 9.14 us  [passed_along(): return lax.ppermute(x, SHARDS, pairs)]
    dot_general x18 -> x0, matrix products: 9.94 us -> none  [the longest x3 3.68 us: body(): jnp.einsum('kgts,skd->tkgd', weights, head_values, preferred_element_type...]
    all_to_all x0 -> x1, blocking collectives: none -> 8.5 us  [exchanged(): return lax.all_to_all(x, 'head', split_axis=0, concat_axis=0, tiled=True)]
    unnamed x42 -> x4, local copies, waits for them, and re-layouts: 7.75 us -> 0.01 us
    pallas_call x0 -> x3, Pallas kernels: none -> 6.75 us  [the longest x1 3.58 us: body(): pl.pallas_call(attention, out_shape=(out(query.shape, query.dtype), out(q...]
    all_to_all x4 -> x0, local copies, waits for them, and re-layouts: 3.43 us -> none  [the longest x1 1.53 us: body(): lax.all_to_all(key, 'head', split_axis=1, concat_axis=0, tiled=True)]
    ppermute x8 -> x4, waiting for transfers between devices: 23.5 us -> 25.4 us  [passed_along(): return lax.ppermute(x, SHARDS, pairs)]
  transfers between devices with their start and end apart: 12 -> 5, of which waited for: 5 -> 5; matrix products, arithmetic and copies ran while one was open for 13% -> 2% of each run, Pallas kernels for 0% -> 0%
where the time goes in v1:
time: 61.4 us; the launch traced here: 60.9 us
  waiting for transfers between devices  28.6 us (47%)
  starting transfers between devices  15.4 us (25%)
  blocking collectives  8.5 us (14%)
  Pallas kernels  6.75 us (11%)
  other arithmetic  1.03 us (2%)
  between operations  0.7 us (1%)
    ppermute x4, waiting for transfers between devices, passed_along(): return lax.ppermute(x, SHARDS, pairs)  25.4 us
    ppermute x4, starting transfers between devices, passed_along(): return lax.ppermute(x, SHARDS, pairs)  9.14 us
    all_to_all x1, blocking collectives, exchanged(): return lax.all_to_all(x, 'head', split_axis=0, concat_axis=0, tiled=True)  8.5 us
    all_to_all x1, starting transfers between devices, exchanged(): return lax.all_to_all(x, 'head', split_axis=0, concat_axis=0, tiled=True)  6.22 us
    pallas_call x1, Pallas kernels, body(): pl.pallas_call(attention, out_shape=(out(query.shape, query.dtype), out(q...  3.58 us
    all_to_all x1, waiting for transfers between devices, exchanged(): return lax.all_to_all(x, 'head', split_axis=0, concat_axis=0, tiled=True)  3.14 us
    pallas_call x1, Pallas kernels, body(): pl.pallas_call(pack, out_shape=out((members, 2, rows, width), key.dtype),...  1.61 us
    pallas_call x1, Pallas kernels, body(): pl.pallas_call(finish, out_shape=(out(key.shape, key.dtype), out(value.sh...  1.56 us
  transfers between devices with their start and end apart: 5, of which 5 were waited for; matrix products, arithmetic and copies ran while one was open for 2% of the time, Pallas kernels for 0%

profile of v1, /device:TPU:56, one launch (start us, length us, event | category | flops | bytes accessed | tf_op | source)
XLA Modules:
  0.0 60.9 jit_solution(3465177532132715689)
XLA Ops:
  0.6 0.0 copy-start.1
  0.6 0.0 copy-start
  0.7 1.6 %pack.1 = bf16[4,2,32,256]{3,2,1,0:T(8,128)(2,1)} custom-call(bf16[32,1024]{1,0:T(8,128)(2,1)} %k_ref.1, bf16[32,1024]{1,0:T(8,128)(2,1)} %v_ref.1), custom_call_target="tpu_custom_call" | custom-call | tf_op jit(solution)/shard_map/pack/pallas_call | solution.py:115
  2.3 6.2 %all-to-all-start = ((bf16[4,2,32,256]{3,2,1,0:T(8,128)(2,1)}), bf16[4,2,32,256]{3,2,1,0:T(8,128)(2,1)S(1)}, u32[]{:S(2)}, u32[]{:S(2)}) async-start(bf16[4,2,32,256]{3,2,1,0:T(8,128)(2,1)} %pack.1), calls=%async_computation | async-start | bytes 262144 | tf_op jit(solution)/shard_map/all_to_all | solution.py:29
  8.5 0.8 %broadcast_select_fusion.1 = (s32[128]{0:T(128)S(1)}, s32[128]{0:T(128)S(1)}, s32[128]{0:T(128)S(1)}) fusion(pred[]{:T(512)S(6)} %ge.10, s32[24576]{0:T(1024)} %param.9, s32[]{:T(128)S(6)} %select_n.48, s32[]{:T(128)S(6)} %select_n.45, pred[]{:T(512)S(6)} %ge.9, s32[]{:T(128)S(6)} %select_n.52, pred[]{:T(512)S(6)} %ge.11), kind=kLoop, calls=%fused_computation.6 | loop fusion | flops 384 | bytes 3087 | tf_op jit(solution)/shard_map/jit(_where)/select_n | solution.py:131
  9.3 3.1 %all-to-all-done.kv0_ref = bf16[4,2,32,256]{3,2,1,0:T(8,128)(2,1)S(1)} async-done(((bf16[4,2,32,256]{3,2,1,0:T(8,128)(2,1)}), bf16[4,2,32,256]{3,2,1,0:T(8,128)(2,1)S(1)}, u32[]{:S(2)}, u32[]{:S(2)}) %all-to-all-start) | async-done | bytes 131104 | tf_op jit(solution)/shard_map/all_to_all | solution.py:29
  12.5 3.4 %collective-permute-start.1 = (bf16[4,2,32,256]{3,2,1,0:T(8,128)(2,1)S(1)}, bf16[4,2,32,256]{3,2,1,0:T(8,128)(2,1)S(1)}, u32[]{:S(2)}, u32[]{:S(2)}) collective-permute-start(bf16[4,2,32,256]{3,2,1,0:T(8,128)(2,1)S(1)} %all-to-all-done.kv0_ref), channel_id=1, source_target_pairs={{0,8},{4,12},{8,16},{12,20},{16,24},{20,28},{24,32},{28,36},{32,40... | collective-permute-start | bytes 393224 | tf_op jit(solution)/shard_map/ppermute | solution.py:25
  15.8 1.9 %collective-permute-start = (bf16[4,2,32,256]{3,2,1,0:T(8,128)(2,1)S(1)}, bf16[4,2,32,256]{3,2,1,0:T(8,128)(2,1)S(1)}, u32[]{:S(2)}, u32[]{:S(2)}) collective-permute-start(bf16[4,2,32,256]{3,2,1,0:T(8,128)(2,1)S(1)} %all-to-all-done.kv0_ref), channel_id=1, source_target_pairs={{0,4},{4,8},{8,12},{12,16},{16,20},{20,24},{24,28},{28,32},{32,36}... | collective-permute-start | bytes 393224 | tf_op jit(solution)/shard_map/ppermute | solution.py:25
  17.8 0.1 select_compare_fusion
  17.9 19.0 %collective-permute-done.1.kv2_ref = bf16[4,2,32,256]{3,2,1,0:T(8,128)(2,1)S(1)} collective-permute-done((bf16[4,2,32,256]{3,2,1,0:T(8,128)(2,1)S(1)}, bf16[4,2,32,256]{3,2,1,0:T(8,128)(2,1)S(1)}, u32[]{:S(2)}, u32[]{:S(2)}) %collective-permute-start.1) | collective-permute-done | bytes 131104 | tf_op jit(solution)/shard_map/ppermute | solution.py:25
  37.0 0.5 collective-permute-done.kv1_ref
  37.5 0.0 copy-done.1
  37.5 0.0 copy-done
  37.5 3.6 %attention.1 = (bf16[128,1536]{1,0:T(8,128)(2,1)}, bf16[128,1536]{1,0:T(8,128)(2,1)}, f32[4,2,32,256]{3,2,1,0:T(8,128)S(1)}, bf16[4,2,32,256]{3,2,1,0:T(8,128)(2,1)S(1)}, bf16[4,2,32,256]{3,2,1,0:T(8,128)(2,1)S(1)}) custom-call(bf16[128,1536]{1,0:T(8,128)(2,1)S(1)} %copy-done, bf16[128,1536]{1,0:T(8,128)(2,1)S(1)} %copy-done.1, ...), custom_call_target="tpu_custom_call" | custom-call | tf_op jit(solution)/shard_map/attention/pallas_call | solution.py:143
  41.1 1.9 %collective-permute-start.2 = (bf16[4,2,32,256]{3,2,1,0:T(8,128)(2,1)S(1)}, bf16[4,2,32,256]{3,2,1,0:T(8,128)(2,1)S(1)}, u32[]{:S(2)}, u32[]{:S(2)}) collective-permute-start(bf16[4,2,32,256]{3,2,1,0:T(8,128)(2,1)S(1)} %get-tuple-element.14), channel_id=1, source_target_pairs={{4,0},{8,4},{12,8},{16,12},{20,16},{24,20},{28,24},{32,28},{36,32}... | collective-permute-start | bytes 393224 | tf_op jit(solution)/shard_map/ppermute | solution.py:25
  43.0 1.9 %collective-permute-start.3 = (bf16[4,2,32,256]{3,2,1,0:T(8,128)(2,1)S(1)}, bf16[4,2,32,256]{3,2,1,0:T(8,128)(2,1)S(1)}, u32[]{:S(2)}, u32[]{:S(2)}) collective-permute-start(bf16[4,2,32,256]{3,2,1,0:T(8,128)(2,1)S(1)} %get-tuple-element.15), channel_id=1, source_target_pairs={{8,0},{12,4},{16,8},{20,12},{24,16},{28,20},{32,24},{36,28},{40,32... | collective-permute-start | bytes 393224 | tf_op jit(solution)/shard_map/ppermute | solution.py:25
  44.9 0.6 collective-permute-done.2
  45.5 5.3 %collective-permute-done.3 = bf16[4,2,32,256]{3,2,1,0:T(8,128)(2,1)S(1)} collective-permute-done((bf16[4,2,32,256]{3,2,1,0:T(8,128)(2,1)S(1)}, bf16[4,2,32,256]{3,2,1,0:T(8,128)(2,1)S(1)}, u32[]{:S(2)}, u32[]{:S(2)}) %collective-permute-start.3) | collective-permute-done | bytes 131104 | tf_op jit(solution)/shard_map/ppermute | solution.py:25
  50.8 0.1 add_convert_fusion
  50.9 8.5 %all_to_all.10.x_ref = bf16[4,2,32,256]{3,2,1,0:T(8,128)(2,1)} all-to-all(bf16[4,2,32,256]{3,2,1,0:T(8,128)(2,1)S(1)} %add_convert_fusion), channel_id=1, replica_groups=mesh['outer'=24,'inner'=8,'head'=4] {'head'}, dimensions={0} | all-to-all | bytes 262144 | tf_op jit(solution)/shard_map/all_to_all | solution.py:29
  59.4 1.6 %finish.1 = (bf16[32,1024]{1,0:T(8,128)(2,1)}, bf16[32,1024]{1,0:T(8,128)(2,1)}) custom-call(bf16[4,2,32,256]{3,2,1,0:T(8,128)(2,1)} %all_to_all.10.x_ref), custom_call_target="tpu_custom_call" | custom-call | tf_op jit(solution)/shard_map/finish/pallas_call | solution.py:162
  (1 shorter events, 0.0 us)
Async XLA Ops:
  0.6 36.9 %copy-start.1 = (bf16[128,1536]{1,0:T(8,128)(2,1)S(1)}, bf16[128,1536]{1,0:T(8,128)(2,1)}, u32[]{:S(2)}) copy-start(bf16[128,1536]{1,0:T(8,128)(2,1)} %g_ref.1) | copy-start | bytes 1179652
  0.6 36.9 %copy-start = (bf16[128,1536]{1,0:T(8,128)(2,1)S(1)}, bf16[128,1536]{1,0:T(8,128)(2,1)}, u32[]{:S(2)}) copy-start(bf16[128,1536]{1,0:T(8,128)(2,1)} %q_ref.1) | copy-start | bytes 1179652
  2.3 10.2 %all-to-all-start = ((bf16[4,2,32,256]{3,2,1,0:T(8,128)(2,1)}), bf16[4,2,32,256]{3,2,1,0:T(8,128)(2,1)S(1)}, u32[]{:S(2)}, u32[]{:S(2)}) async-start(bf16[4,2,32,256]{3,2,1,0:T(8,128)(2,1)} %pack.1), calls=%async_computation | async-start | bytes 262144 | tf_op jit(solution)/shard_map/all_to_all | solution.py:29
  12.5 24.5 %collective-permute-start.1 = (bf16[4,2,32,256]{3,2,1,0:T(8,128)(2,1)S(1)}, bf16[4,2,32,256]{3,2,1,0:T(8,128)(2,1)S(1)}, u32[]{:S(2)}, u32[]{:S(2)}) collective-permute-start(bf16[4,2,32,256]{3,2,1,0:T(8,128)(2,1)S(1)} %all-to-all-done.kv0_ref), channel_id=1, source_target_pairs={{0,8},{4,12},{8,16},{12,20},{16,24},{20,28},{24,32},{28,36},{32,40... | collective-permute-start | bytes 393224 | tf_op jit(solution)/shard_map/ppermute | solution.py:25
  15.8 21.7 %collective-permute-start = (bf16[4,2,32,256]{3,2,1,0:T(8,128)(2,1)S(1)}, bf16[4,2,32,256]{3,2,1,0:T(8,128)(2,1)S(1)}, u32[]{:S(2)}, u32[]{:S(2)}) collective-permute-start(bf16[4,2,32,256]{3,2,1,0:T(8,128)(2,1)S(1)} %all-to-all-done.kv0_ref), channel_id=1, source_target_pairs={{0,4},{4,8},{8,12},{12,16},{16,20},{20,24},{24,28},{28,32},{32,36}... | collective-permute-start | bytes 393224 | tf_op jit(solution)/shard_map/ppermute | solution.py:25
  41.1 4.4 %collective-permute-start.2 = (bf16[4,2,32,256]{3,2,1,0:T(8,128)(2,1)S(1)}, bf16[4,2,32,256]{3,2,1,0:T(8,128)(2,1)S(1)}, u32[]{:S(2)}, u32[]{:S(2)}) collective-permute-start(bf16[4,2,32,256]{3,2,1,0:T(8,128)(2,1)S(1)} %get-tuple-element.14), channel_id=1, source_target_pairs={{4,0},{8,4},{12,8},{16,12},{20,16},{24,20},{28,24},{32,28},{36,32}... | collective-permute-start | bytes 393224 | tf_op jit(solution)/shard_map/ppermute | solution.py:25
  43.0 7.8 %collective-permute-start.3 = (bf16[4,2,32,256]{3,2,1,0:T(8,128)(2,1)S(1)}, bf16[4,2,32,256]{3,2,1,0:T(8,128)(2,1)S(1)}, u32[]{:S(2)}, u32[]{:S(2)}) collective-permute-start(bf16[4,2,32,256]{3,2,1,0:T(8,128)(2,1)S(1)} %get-tuple-element.15), channel_id=1, source_target_pairs={{8,0},{12,4},{16,8},{20,12},{24,16},{28,20},{32,24},{36,28},{40,32... | collective-permute-start | bytes 393224 | tf_op jit(solution)/shard_map/ppermute | solution.py:25
